TPU v7x, 256 devices: a whole 4x4x8 slice. The times are simulated.
256 devices in a mesh: depth: 8 (over y, core), tile: 32 (over x, z).
Axes of the slice: x: 4, y: 4, z: 8, core: 2. Of those that a mesh axis runs over, the one named last changes fastest.
Arguments:
- density: int32 [256, 2048, 1024], P('depth', 'tile'), may hold values from 0 to 255
- view_flip: int32 [32], P('tile'), may hold values from 0 to 1
- tf_coeff: float32 [4, 4], replicated, may hold values from -4 to 4
Outputs:
- shaded: float32 [3, 2048, 1024], P(None, 'tile', 'depth')
All inputs are finite; a program needn't handle non-finite values.
Results may differ from a plain program's by a relative error of at most 0.0003.
Values may be sent and summed in bfloat16 or wider, within the bound.
A program may use at most 192 MiB of HBM per device.

v0:
```python
import jax
import jax.numpy as jnp
from jax import lax
from jax.sharding import PartitionSpec as P

RADIUS = 8


opacity_scale = 0.008
grad_half = 1.0
light_x = 0.48
light_y = 0.6
light_z = 0.64
spatial_scale = 1.0 / 72.0
depth_weight = 20.0
normal_weight = 2.0


def with_halo(shard, sides, width):
    for axis, dim in sides:
        count, length = (lax.axis_size(axis), shard.shape[dim])
        up = [(i, (i + 1) % count) for i in range(count - 1)]
        down = [(j, i) for i, j in up]
        last = lax.slice_in_dim(shard, length - width, length, axis=dim)
        first = lax.slice_in_dim(shard, 0, width, axis=dim)
        before = lax.ppermute(last, axis, up)
        after = lax.ppermute(first, axis, down)
        shard = jnp.concatenate([before, shard, after], axis=dim)
    return shard


def swapped(block, axis, stride):
    count = lax.axis_size(axis)
    route = []
    for low in range(count):
        high = low | 1 << stride
        if high != low and high < count:
            route += [(low, high), (high, low)]
    return lax.ppermute(block, axis, route)


def polynomial(coeff, scaled):
    return coeff[0] + scaled * (coeff[1] + scaled * (coeff[2] + scaled * coeff[3]))


def integrate(field, flipped, tf_coeff, depth_start, depth_total):
    centre = field[1:-1, 1:-1, :]
    sideways = jnp.pad(centre, ((0, 0), (0, 0), (1, 1)))
    grad_x = (sideways[:, :, 2:] - sideways[:, :, :-2]) * grad_half
    grad_y = (field[1:-1, 2:, :] - field[1:-1, :-2, :]) * grad_half
    grad_z = (field[2:, 1:-1, :] - field[:-2, 1:-1, :]) * grad_half
    scaling = lax.rsqrt(1.0 + grad_x * grad_x + grad_y * grad_y + grad_z * grad_z)
    normal_x = grad_x * scaling
    normal_y = grad_y * scaling
    normal_z = grad_z * scaling
    shading = 0.35 + 0.65 * jnp.abs(light_x * normal_x + light_y * normal_y + light_z * normal_z)
    scaled = 2.0 * centre - 1.0
    sigma = opacity_scale * jax.nn.softplus(polynomial(tf_coeff[0], scaled))
    running = jnp.cumsum(sigma, axis=0)
    total = running[-1]
    optical = jnp.where(flipped == 1, total - running, running - sigma)
    weight = jnp.exp(-optical) * (1.0 - jnp.exp(-sigma))
    cells = sigma.shape[0]
    height = (
        (depth_start + jnp.arange(cells, dtype=jnp.int32)).astype(jnp.float32) + 0.5
    ) / depth_total
    height = jnp.where(flipped == 1, 1.0 - height, height)[:, None, None]
    planes = []
    for channel in range(1, 4):
        colour = jax.nn.sigmoid(polynomial(tf_coeff[channel], scaled)) * shading
        planes.append(jnp.sum(weight * colour, axis=0))
    planes.append(1.0 - jnp.exp(-total))
    planes.append(jnp.sum(weight * height, axis=0))
    planes.append(jnp.sum(weight * normal_x, axis=0))
    planes.append(jnp.sum(weight * normal_y, axis=0))
    planes.append(jnp.sum(weight * normal_z, axis=0))
    return jnp.stack(planes, axis=0)


def shade_image(extended, rows, cols):
    colour = extended[0:3]
    normal = extended[5:8]
    facing = jnp.maximum(light_x * normal[0] + light_y * normal[1] + light_z * normal[2], 0.0)
    lit = colour * (0.4 + 0.6 * facing)
    stacked = jnp.concatenate([extended, lit], axis=0)
    centre = extended[:, RADIUS : RADIUS + rows, RADIUS : RADIUS + cols]
    span = 2 * RADIUS + 1

    def row_step(offset_y, sums):
        numer, denom = sums
        offset_y = offset_y.astype(jnp.int32)
        rise = (offset_y - RADIUS).astype(jnp.float32)
        for offset_x in range(span):
            near = lax.dynamic_slice(
                stacked, (jnp.int32(0), offset_y, jnp.int32(offset_x)), (11, rows, cols)
            )
            run = float(offset_x - RADIUS)
            exponent = -(rise * rise + run * run) * spatial_scale
            exponent = exponent - depth_weight * (centre[4] - near[4]) ** 2
            exponent = exponent - normal_weight * jnp.sum((centre[5:8] - near[5:8]) ** 2, axis=0)
            weight = near[3] * jnp.exp(exponent)
            numer = numer + weight * near[8:11]
            denom = denom + weight
        return (numer, denom)

    start = (jnp.zeros((3, rows, cols), jnp.float32), jnp.zeros((rows, cols), jnp.float32))
    numer, denom = lax.fori_loop(0, span, row_step, start)
    return numer / (1.0 + denom)


def over_layer(front, back):
    return front + (1.0 - front[3:4]) * back


def reverse_bits(value, rounds):
    result = 0
    for level in range(rounds):
        result = result * 2 + (value >> level) % 2
    return result


def per_device(density, view_flip, tf_coeff):
    depth_cells, rows, width = density.shape
    count = lax.axis_size("depth")
    position = lax.axis_index("depth")
    flipped = view_flip[0]
    levels = density.astype(jnp.bfloat16)
    extended = with_halo(levels, (("depth", 0), ("tile", 1)), 1)
    field = extended.astype(jnp.float32) / 255.0
    planes = integrate(field, flipped, tf_coeff, position * depth_cells, depth_cells * count)
    columns = width // count
    blocks = planes.reshape(8, rows, count, columns)
    rounds = count.bit_length() - 1
    current = jnp.concatenate(
        [
            blocks[:, :, reverse_bits(place, rounds) : reverse_bits(place, rounds) + 1]
            for place in range(count)
        ],
        axis=2,
    )
    for level in range(rounds):
        half = current.shape[2] // 2
        upper = position // 2**level % 2
        kept = lax.dynamic_slice_in_dim(current, upper * half, half, 2)
        given = lax.dynamic_slice_in_dim(current, (1 - upper) * half, half, 2)
        partner = swapped(given, "depth", level)
        leading = upper == flipped
        front = jnp.where(leading, kept, partner)
        back = jnp.where(leading, partner, kept)
        current = over_layer(front, back)
    composite = current[:, :, 0]
    bordered = with_halo(composite, (("depth", 2), ("tile", 1)), RADIUS)
    return shade_image(bordered, rows, columns)


def solution(mesh):
    in_specs = (P("depth", "tile", None), P("tile"), P())
    out_specs = P(None, "tile", "depth")
    return jax.shard_map(
        per_device, mesh=mesh, in_specs=in_specs, out_specs=out_specs, check_vma=False
    )
```

profile of v0, /device:TPU:15, one launch (start us, length us, event | category | flops | bytes accessed | tf_op | source)
XLA Modules:
  0.0 227.1 jit_solution(1818797018401699545)
XLA Ops:
  0.0 4.6 %convert_element_type.25 = bf16[32,64,1024]{2,1,0:T(8,128)(2,1)S(1)} convert(s32[32,64,1024]{2,1,0:T(8,128)} %param.5) | non-fusion elementwise | flops 2097152 | bytes 12582912 | tf_op jit(solution)/shard_map/convert_element_type | solution.py:127
  4.7 1.9 copy-done.1
  6.6 3.8 %collective-permute-start = (bf16[1,64,1024]{2,1,0:T(8,128)(2,1)S(1)}, bf16[1,64,1024]{2,1,0:T(8,128)(2,1)S(1)}, u32[]{:S(2)}, u32[]{:S(2)}) collective-permute-start(bf16[1,64,1024]{2,1,0:T(8,128)(2,1)S(1)} %get-tuple-element.217), channel_id=1, source_target_pairs={{0,32},{32,64},{64,96},{96,128},{128,160},{160,192},{192,224},{1,3... | collective-permute-start | bytes 393224 | tf_op jit(solution)/shard_map/ppermute | solution.py:26
  10.4 1.9 collective-permute-start.1
  13.0 0.7 fusion.223
  13.7 3.0 %collective-permute-done.1 = bf16[1,64,1024]{2,1,0:T(8,128)(2,1)S(1)} collective-permute-done((bf16[1,64,1024]{2,1,0:T(8,128)(2,1)S(1)}, bf16[1,64,1024]{2,1,0:T(8,128)(2,1)S(1)}, u32[]{:S(2)}, u32[]{:S(2)}) %collective-permute-start.1) | collective-permute-done | bytes 131104 | tf_op jit(solution)/shard_map/ppermute | solution.py:27
  16.6 1.4 pad_maximum_fusion.4
  18.1 3.5 %collective-permute-start.2 = (bf16[34,1,1024]{2,1,0:T(2,128)(2,1)S(1)}, bf16[34,1,1024]{2,1,0:T(2,128)(2,1)S(1)}, u32[]{:S(2)}, u32[]{:S(2)}) collective-permute-start(bf16[34,1,1024]{2,1,0:T(2,128)(2,1)S(1)} %get-tuple-element.215), channel_id=1, source_target_pairs={{0,1},{1,2},{2,3},{3,4},{4,5},{5,6},{6,7},{7,8},{8,9},{9,10},{10,1... | collective-permute-start | bytes 208904 | tf_op jit(solution)/shard_map/ppermute | solution.py:26
  21.6 6.1 %collective-permute-start.3 = (bf16[34,1,1024]{2,1,0:T(2,128)(2,1)S(1)}, bf16[34,1,1024]{2,1,0:T(2,128)(2,1)S(1)}, u32[]{:S(2)}, u32[]{:S(2)}) collective-permute-start(bf16[34,1,1024]{2,1,0:T(2,128)(2,1)S(1)} %get-tuple-element.216), channel_id=1, source_target_pairs={{1,0},{2,1},{3,2},{4,3},{5,4},{6,5},{7,6},{8,7},{9,8},{10,9},{11,1... | collective-permute-start | bytes 208904 | tf_op jit(solution)/shard_map/ppermute | solution.py:27
  27.8 0.8 collective-permute-done.2
  28.6 1.8 collective-permute-done.3
  30.4 4.7 %convert_multiply_fusion = f32[34,66,1024]{2,1,0:T(8,128)S(1)} fusion(bf16[34,1,1024]{2,1,0:T(2,128)(2,1)S(1)} %collective-permute-done.3, bf16[1,64,1024]{2,1,0:T(8,128)(2,1)S(1)} %collective-permute-done.1, bf16[32,64,1024]{2,1,0:T(8,128)(2,1)} %copy-done.1, bf16[1,64,1024]{2,1,0:T(8,128)(2,1)S(1)} %collective-permute-done, ...), kind=kLoop, calls=%fused_computation.290 | loop fusion | flops 25276416 | bytes 13787136 | tf_op jit(solution)/shard_map/div | solution.py:129
  35.1 4.9 %slice.1032 = f32[32,64,1024]{2,1,0:T(8,128)} slice(f32[34,66,1024]{2,1,0:T(8,128)S(1)} %convert_multiply_fusion), slice={[1:33], [1:65], [0:1024]} | slice | bytes 16777216 | tf_op jit(solution)/shard_map/slice | solution.py:47
  40.0 1.4 copy-done
  41.4 10.1 %fusion.216 = f32[32,64,1024]{2,1,0:T(8,128)S(1)} fusion(f32[]{:T(128)} %bitcast.4, f32[]{:T(128)} %bitcast.3, f32[]{:T(128)} %bitcast.2, f32[]{:T(128)} %bitcast.1, f32[34,66,1024]{2,1,0:T(8,128)S(1)} %convert_multiply_fusion), kind=kOutput, calls=%fused_computation.355 | output fusion | flops 96468992 | bytes 16777232 | tf_op jit(solution)/shard_map/jit(cumsum)/reduce_window_sum | solution.py:59
  51.5 3.3 %copy-done.2 = f32[32,64,1024]{2,1,0:T(8,128)} copy-done((f32[32,64,1024]{2,1,0:T(8,128)}, f32[32,64,1024]{2,1,0:T(8,128)S(1)}, u32[]{:S(2)}) %copy-start.2) | copy-done | bytes 8388632
  54.9 41.0 %multiply_reduce_fusion = (f32[64,1024]{1,0:T(8,128)S(1)}, f32[64,1024]{1,0:T(8,128)S(1)}, f32[64,1024]{1,0:T(8,128)S(1)}, f32[64,1024]{1,0:T(8,128)S(1)}, f32[3...) fusion(f32[32]{0:T(128)S(1)} %broadcast_select_fusion.3, ...), kind=kLoop, calls=%fused_computation.297 | loop fusion | flops 87818240 | bytes 93585552 | tf_op jit(solution)/shard_map/reduce_sum | solution.py:76
  95.9 28.9 %multiply_reduce_fusion.4 = (f32[64,1024]{1,0:T(8,128)S(1)}, f32[64,1024]{1,0:T(8,128)S(1)}, f32[64,1024]{1,0:T(8,128)S(1)}) fusion(f32[32,64,1024]{2,1,0:T(8,128)} %get-tuple-element.194, f32[]{:T(128)} %bitcast.17, f32[]{:T(128)} %bitcast.16, f32[]{:T(128)} %bitcast.15, f32[]{:T(128)} %bitcast.14, f32[34,66,1024]{2,1,0:T(8,128)} %copy-done, f32[]{:T(128)} %bitcast.13, ...), kind=kLoop, calls=%fused_computation.301 | loop fusion | flops 115146752 | bytes 42729520 | tf_op jit(solution)/shard_map/reduce_sum | solution.py:71
  125.5 2.8 %fusion.221 = (f32[8,64,1,128]{3,2,1,0:T(1,128)S(1)}, f32[8,64,1,128]{3,2,1,0:T(1,128)S(1)}, f32[8,64,1,128]{3,2,1,0:T(1,128)S(1)}, f32[8,64,1,128]{3,2,1,0:T(1,...) fusion(f32[8,64,8,128]{3,2,1,0:T(8,128)S(1)} %bitcast_dynamic-u, ...), kind=kLoop, calls=%fused_computation.358 | loop fusion | bytes 4194304 | tf_op jit(solution)/shard_map/slice | solution.py:136
  128.3 5.1 %concatenate.21 = f32[8,64,8,128]{3,2,1,0:T(8,128)S(1)} concatenate(f32[8,64,1,128]{3,2,1,0:T(1,128)} %get-tuple-element.226, f32[8,64,1,128]{3,2,1,0:T(1,128)} %get-tuple-element.225, f32[8,64,1,128]{3,2,1,0:T(1,128)} %get-tuple-element.224, f32[8,64,1,128]{3,2,1,0:T(1,128)S(1)} %get-tuple-element.223, f32[8,64,1,128]{3,2,1,0:T(1,128)S(1)} %get-tuple-element.222, ...), dimensions={2} | concatenate | bytes 4194304 | tf_op jit(solution)/shard_map/concatenate | solution.py:134
  133.4 1.2 constant_dynamic-slice_fusion.2
  134.6 2.9 %collective-permute-done.4 = f32[8,64,4,128]{3,2,1,0:T(4,128)S(1)} collective-permute-done((f32[8,64,4,128]{3,2,1,0:T(4,128)}, f32[8,64,4,128]{3,2,1,0:T(4,128)S(1)}, u32[]{:S(2)}, u32[]{:S(2)}) %collective-permute-start.4) | collective-permute-done | bytes 1048608 | tf_op jit(solution)/shard_map/ppermute | solution.py:39
  137.7 0.7 copy-done.3
  138.4 1.6 multiply_add_fusion.2
  140.5 13.3 %collective-permute-done.5 = f32[8,64,2,128]{3,2,1,0:T(2,128)S(1)} collective-permute-done((f32[8,64,2,128]{3,2,1,0:T(2,128)S(1)}, f32[8,64,2,128]{3,2,1,0:T(2,128)S(1)}, u32[]{:S(2)}, u32[]{:S(2)}) %collective-permute-start.5) | collective-permute-done | bytes 524320 | tf_op jit(solution)/shard_map/ppermute | solution.py:39
  154.9 1.4 collective-permute-start.6
  156.3 7.1 %collective-permute-done.6 = f32[8,64,1,128]{3,2,1,0:T(1,128)S(1)} collective-permute-done((f32[8,64,1,128]{3,2,1,0:T(1,128)S(1)}, f32[8,64,1,128]{3,2,1,0:T(1,128)S(1)}, u32[]{:S(2)}, u32[]{:S(2)}) %collective-permute-start.6) | collective-permute-done | bytes 262176 | tf_op jit(solution)/shard_map/ppermute | solution.py:39
  164.3 5.0 %collective-permute-start.7 = (f32[8,64,8]{2,1,0:T(8,128)S(1)}, f32[8,64,8]{2,1,0:T(8,128)S(1)}, u32[]{:S(2)}, u32[]{:S(2)}) collective-permute-start(f32[8,64,8]{2,1,0:T(8,128)S(1)} %get-tuple-element.229), channel_id=1, source_target_pairs={{0,32},{32,64},{64,96},{96,128},{128,160},{160,192},{192,224},{1,3... | collective-permute-start | bytes 49160 | tf_op jit(solution)/shard_map/ppermute | solution.py:26
  169.3 1.9 collective-permute-start.8
  171.2 1.4 collective-permute-done.7
  172.6 4.4 %collective-permute-done.8 = f32[8,64,8]{2,1,0:T(8,128)S(1)} collective-permute-done((f32[8,64,8]{2,1,0:T(8,128)S(1)}, f32[8,64,8]{2,1,0:T(8,128)S(1)}, u32[]{:S(2)}, u32[]{:S(2)}) %collective-permute-start.8) | collective-permute-done | bytes 16416 | tf_op jit(solution)/shard_map/ppermute | solution.py:27
  177.1 5.9 %collective-permute-start.10 = (f32[8,8,144]{2,1,0:T(8,128)S(1)}, f32[8,8,144]{2,1,0:T(8,128)S(1)}, u32[]{:S(2)}, u32[]{:S(2)}) collective-permute-start(f32[8,8,144]{2,1,0:T(8,128)S(1)} %get-tuple-element.228), channel_id=1, source_target_pairs={{1,0},{2,1},{3,2},{4,3},{5,4},{6,5},{7,6},{8,7},{9,8},{10,9},{11,1... | collective-permute-start | bytes 110600 | tf_op jit(solution)/shard_map/ppermute | solution.py:27
  183.0 1.9 collective-permute-start.9
  184.9 5.3 %collective-permute-done.9 = f32[8,8,144]{2,1,0:T(8,128)S(1)} collective-permute-done((f32[8,8,144]{2,1,0:T(8,128)S(1)}, f32[8,8,144]{2,1,0:T(8,128)S(1)}, u32[]{:S(2)}, u32[]{:S(2)}) %collective-permute-start.9) | collective-permute-done | bytes 36896 | tf_op jit(solution)/shard_map/ppermute | solution.py:26
  191.0 35.5 %while.18 = (s32[]{:T(128)}, f32[3,64,128]{2,1,0:T(8,128)S(1)}, f32[64,128]{1,0:T(8,128)S(1)}, f32[11,80,144]{2,1,0:T(8,128)S(1)}, f32[8,64,128]{2,1,0:T(8,128)S...) while((s32[]{:T(128)}, f32[3,64,128]{2,1,0:T(8,128)S(1)}, ...), condition=%wide.region_26.27_spmd.clone, body=%wide.region_8.26_spmd.clone.sunk | while | flops 4071460 | bytes 8880856 | solution.py:107
  192.5 0.5 fusion.236
  194.6 0.5 fusion.236
  196.7 0.5 fusion.236
  198.8 0.5 fusion.236
  209.2 0.5 fusion.236
  211.3 0.5 fusion.236
  213.4 0.5 fusion.236
  215.5 0.5 fusion.236
  217.6 0.5 fusion.236
  219.7 0.5 fusion.236
  221.8 0.5 fusion.236
  223.8 0.5 fusion.236
  226.4 0.7 broadcast_divide_fusion
  (155 shorter events, 31.9 us)
Async XLA Ops:
  0.0 13.0 %copy-start.4 = (f32[4,4]{1,0:T(4,128)S(1)}, f32[4,4]{1,0:T(4,128)}, u32[]{:S(2)}) copy-start(f32[4,4]{1,0:T(4,128)} %param.7) | copy-start | bytes 196
  4.6 1.9 copy-start.1
  6.6 7.1 %collective-permute-start = (bf16[1,64,1024]{2,1,0:T(8,128)(2,1)S(1)}, bf16[1,64,1024]{2,1,0:T(8,128)(2,1)S(1)}, u32[]{:S(2)}, u32[]{:S(2)}) collective-permute-start(bf16[1,64,1024]{2,1,0:T(8,128)(2,1)S(1)} %get-tuple-element.217), channel_id=1, source_target_pairs={{0,32},{32,64},{64,96},{96,128},{128,160},{160,192},{192,224},{1,3... | collective-permute-start | bytes 393224 | tf_op jit(solution)/shard_map/ppermute | solution.py:26
  10.4 6.3 %collective-permute-start.1 = (bf16[1,64,1024]{2,1,0:T(8,128)(2,1)S(1)}, bf16[1,64,1024]{2,1,0:T(8,128)(2,1)S(1)}, u32[]{:S(2)}, u32[]{:S(2)}) collective-permute-start(bf16[1,64,1024]{2,1,0:T(8,128)(2,1)S(1)} %get-tuple-element.218), channel_id=1, source_target_pairs={{32,0},{64,32},{96,64},{128,96},{160,128},{192,160},{224,192},{33,... | collective-permute-start | bytes 393224 | tf_op jit(solution)/shard_map/ppermute | solution.py:27
  18.1 10.6 %collective-permute-start.2 = (bf16[34,1,1024]{2,1,0:T(2,128)(2,1)S(1)}, bf16[34,1,1024]{2,1,0:T(2,128)(2,1)S(1)}, u32[]{:S(2)}, u32[]{:S(2)}) collective-permute-start(bf16[34,1,1024]{2,1,0:T(2,128)(2,1)S(1)} %get-tuple-element.215), channel_id=1, source_target_pairs={{0,1},{1,2},{2,3},{3,4},{4,5},{5,6},{6,7},{7,8},{8,9},{9,10},{10,1... | collective-permute-start | bytes 208904 | tf_op jit(solution)/shard_map/ppermute | solution.py:26
  21.6 8.8 %collective-permute-start.3 = (bf16[34,1,1024]{2,1,0:T(2,128)(2,1)S(1)}, bf16[34,1,1024]{2,1,0:T(2,128)(2,1)S(1)}, u32[]{:S(2)}, u32[]{:S(2)}) collective-permute-start(bf16[34,1,1024]{2,1,0:T(2,128)(2,1)S(1)} %get-tuple-element.216), channel_id=1, source_target_pairs={{1,0},{2,1},{3,2},{4,3},{5,4},{6,5},{7,6},{8,7},{9,8},{10,9},{11,1... | collective-permute-start | bytes 208904 | tf_op jit(solution)/shard_map/ppermute | solution.py:27
  35.1 6.3 %copy-start = (f32[34,66,1024]{2,1,0:T(8,128)}, f32[34,66,1024]{2,1,0:T(8,128)S(1)}, u32[]{:S(2)}) copy-start(f32[34,66,1024]{2,1,0:T(8,128)S(1)} %convert_multiply_fusion) | copy-start | bytes 27574276
  51.5 3.3 %copy-start.2 = (f32[32,64,1024]{2,1,0:T(8,128)}, f32[32,64,1024]{2,1,0:T(8,128)S(1)}, u32[]{:S(2)}) copy-start(f32[32,64,1024]{2,1,0:T(8,128)S(1)} %fusion.216) | copy-start | bytes 25165828
  134.6 2.9 %collective-permute-start.4 = (f32[8,64,4,128]{3,2,1,0:T(4,128)}, f32[8,64,4,128]{3,2,1,0:T(4,128)S(1)}, u32[]{:S(2)}, u32[]{:S(2)}) collective-permute-start(f32[8,64,4,128]{3,2,1,0:T(4,128)} %constant_dynamic-slice_fusion.2), channel_id=1, source_target_pairs={{0,32},{32,0},{64,96},{96,64},{128,160},{160,128},{192,224},{224,1... | collective-permute-start | bytes 3145736 | tf_op jit(solution)/shard_map/ppermute | solution.py:39
  137.4 1.0 copy-start.3
  140.4 13.5 %collective-permute-start.5 = (f32[8,64,2,128]{3,2,1,0:T(2,128)S(1)}, f32[8,64,2,128]{3,2,1,0:T(2,128)S(1)}, u32[]{:S(2)}, u32[]{:S(2)}) collective-permute-start(f32[8,64,2,128]{3,2,1,0:T(2,128)S(1)} %constant_dynamic-slice_fusion.1), channel_id=1, source_target_pairs={{0,64},{64,0},{32,96},{96,32},{128,192},{192,128},{160,224},{224,1... | collective-permute-start | bytes 1572872 | tf_op jit(solution)/shard_map/ppermute | solution.py:39
  154.9 8.4 %collective-permute-start.6 = (f32[8,64,1,128]{3,2,1,0:T(1,128)S(1)}, f32[8,64,1,128]{3,2,1,0:T(1,128)S(1)}, u32[]{:S(2)}, u32[]{:S(2)}) collective-permute-start(f32[8,64,1,128]{3,2,1,0:T(1,128)S(1)} %constant_dynamic-slice_fusion), channel_id=1, source_target_pairs={{0,128},{128,0},{32,160},{160,32},{64,192},{192,64},{96,224},{224,... | collective-permute-start | bytes 786440 | tf_op jit(solution)/shard_map/ppermute | solution.py:39
  164.3 8.3 %collective-permute-start.7 = (f32[8,64,8]{2,1,0:T(8,128)S(1)}, f32[8,64,8]{2,1,0:T(8,128)S(1)}, u32[]{:S(2)}, u32[]{:S(2)}) collective-permute-start(f32[8,64,8]{2,1,0:T(8,128)S(1)} %get-tuple-element.229), channel_id=1, source_target_pairs={{0,32},{32,64},{64,96},{96,128},{128,160},{160,192},{192,224},{1,3... | collective-permute-start | bytes 49160 | tf_op jit(solution)/shard_map/ppermute | solution.py:26
  169.3 7.7 %collective-permute-start.8 = (f32[8,64,8]{2,1,0:T(8,128)S(1)}, f32[8,64,8]{2,1,0:T(8,128)S(1)}, u32[]{:S(2)}, u32[]{:S(2)}) collective-permute-start(f32[8,64,8]{2,1,0:T(8,128)S(1)} %get-tuple-element.230), channel_id=1, source_target_pairs={{32,0},{64,32},{96,64},{128,96},{160,128},{192,160},{224,192},{33,... | collective-permute-start | bytes 49160 | tf_op jit(solution)/shard_map/ppermute | solution.py:27
  177.1 7.8 %collective-permute-start.10 = (f32[8,8,144]{2,1,0:T(8,128)S(1)}, f32[8,8,144]{2,1,0:T(8,128)S(1)}, u32[]{:S(2)}, u32[]{:S(2)}) collective-permute-start(f32[8,8,144]{2,1,0:T(8,128)S(1)} %get-tuple-element.228), channel_id=1, source_target_pairs={{1,0},{2,1},{3,2},{4,3},{5,4},{6,5},{7,6},{8,7},{9,8},{10,9},{11,1... | collective-permute-start | bytes 110600 | tf_op jit(solution)/shard_map/ppermute | solution.py:27
  183.0 7.3 %collective-permute-start.9 = (f32[8,8,144]{2,1,0:T(8,128)S(1)}, f32[8,8,144]{2,1,0:T(8,128)S(1)}, u32[]{:S(2)}, u32[]{:S(2)}) collective-permute-start(f32[8,8,144]{2,1,0:T(8,128)S(1)} %get-tuple-element.227), channel_id=1, source_target_pairs={{0,1},{1,2},{2,3},{3,4},{4,5},{5,6},{6,7},{7,8},{8,9},{9,10},{10,1... | collective-permute-start | bytes 110600 | tf_op jit(solution)/shard_map/ppermute | solution.py:26
where the time goes:
time: 228 us; the launch traced here: 227 us
  other arithmetic  130 us (57%)
  waiting for transfers between devices  39.9 us (18%)
  starting transfers between devices  31.5 us (14%)
  local copies, waits for them, and re-layouts  23.2 us (10%)
    reduce_sum x1, other arithmetic, integrate(): planes.append(jnp.sum(weight * normal_z, axis=0))  41 us
    reduce_sum x1, other arithmetic, integrate(): planes.append(jnp.sum(weight * colour, axis=0))  28.9 us
    ppermute x3, waiting for transfers between devices, swapped(): return lax.ppermute(block, axis, route)  23.3 us
    ppermute x4, starting transfers between devices, with_halo(): after = lax.ppermute(first, axis, down)  15.8 us
    ppermute x4, starting transfers between devices, with_halo(): before = lax.ppermute(last, axis, up)  14.2 us
    mul x68, other arithmetic, row_step(): numer = numer + weight * near[8:11]  10.3 us
    another operation x1, other arithmetic, integrate(): running = jnp.cumsum(sigma, axis=0)  10.1 us
    ppermute x4, waiting for transfers between devices, with_halo(): after = lax.ppermute(first, axis, down)  9.12 us
  transfers between devices with their start and end apart: 11, of which 9 were waited for; matrix products, arithmetic and copies ran while one was open for 0% of the time, Pallas kernels for 0%

commit v1 on v0

v1 whole, which is shorter than its diff:
```python
import jax
import jax.numpy as jnp
from jax import lax
from jax.experimental import pallas as pl
from jax.experimental.pallas import tpu as pltpu
from jax.sharding import PartitionSpec as P

f32 = jnp.float32
LOG2E = 1.4426950408889634
LIGHT = (0.48, 0.6, 0.64)
RADIUS = 8
SPAN = 2 * RADIUS + 1
BANDS = 2
CHUNKS = 4


def rows_at(start, count=8):
    return pl.ds(pl.multiple_of(start, 8), count)


def poly(a, x):
    return a[0] + x * (a[1] + x * (a[2] + x * a[3]))


def level_coeffs(tf):
    s = 2.0 / 255.0
    table = []
    for q in range(4):
        c0, c1, c2, c3 = (tf[q, i] for i in range(4))
        m = LOG2E if q == 0 else 0.5
        table.append(
            (
                (c0 - c1 + c2 - c3) * m,
                (c1 - 2.0 * c2 + 3.0 * c3) * (s * m),
                (c2 - 3.0 * c3) * (s * s * m),
                c3 * (s * s * s * m),
            )
        )
    return table


def kernel(flip_ref, tf_ref, dens, out_ref, raw, fld, gxs, zh, rh, outb, mine, sibr, parts, feat, pk, hw, he, shf,
           load_sem, zs, zr, rs, rr, ss, sr, cs, cr, hs, hr):
    nd, nt = 8, 32
    d, t = lax.axis_index("depth"), lax.axis_index("tile")
    core, chip = d % 2, d // 2
    flip = flip_ref[0]
    flipped = flip == 1
    cells = dens.shape[0]
    per = cells // CHUNKS
    up_d, dn_d = (d + 1) % nd, (d + nd - 1) % nd
    up_t, dn_t = (t + 1) % nt, (t + nt - 1) % nt
    sib = 2 * chip + 1 - core

    loads = []
    for c in range(CHUNKS):
        piece = pl.ds(c * per, per)
        loads.append(pltpu.make_async_copy(dens.at[piece], raw.at[piece], load_sem.at[c]))
        loads[-1].start()

    barrier = pltpu.get_barrier_semaphore()
    near = [{"depth": up_d}, {"depth": dn_d}, {"tile": up_t}, {"tile": dn_t}]
    near += [{"depth": a, "tile": b} for a in (up_d, dn_d) for b in (up_t, dn_t)]
    near += [{"depth": (d + 2 * e) % nd} for e in (1, 2, 3)]
    for who in near:
        pl.semaphore_signal(barrier, inc=1, device_id=who, device_id_type=pl.DeviceIdType.MESH)
    pl.semaphore_wait(barrier, len(near))

    def remote(src, dst, send, recv, who):
        return pltpu.make_async_remote_copy(src_ref=src, dst_ref=dst, send_sem=send, recv_sem=recv, device_id=who,
                                            device_id_type=pl.DeviceIdType.MESH)

    edge = [
        remote(dens.at[cells - 1], zh.at[0], zs.at[0], zr.at[0], {"depth": up_d}),
        remote(dens.at[0], zh.at[1], zs.at[1], zr.at[1], {"depth": dn_d}),
        remote(dens.at[:, pl.ds(63, 1)], rh.at[0], rs.at[0], rr.at[0], {"tile": up_t}),
        remote(dens.at[:, pl.ds(0, 1)], rh.at[1], rs.at[1], rr.at[1], {"tile": dn_t}),
    ]
    for copy in edge:
        copy.start()

    lane = lax.broadcasted_iota(jnp.int32, (8, 128), 1)

    def prepare(z, carry):
        for g in range(8):
            v = [raw[z, 8 * g : 8 * g + 8, 128 * j : 128 * j + 128].astype(f32) for j in range(8)]
            zero = jnp.zeros((8, 128), f32)
            for j in range(8):
                right = v[j + 1] if j < 7 else zero
                left = v[j - 1] if j > 0 else zero
                hi = pltpu.roll(jnp.where(lane == 0, right, v[j]), 127, 1)
                lo = pltpu.roll(jnp.where(lane == 127, left, v[j]), 1, 1)
                fld[z + 1, j, 8 * g + 8 : 8 * g + 16, :] = v[j]
                gxs[z, j, 8 * g : 8 * g + 8, :] = hi - lo
        return carry

    for c in range(CHUNKS):
        loads[c].wait()
        lax.fori_loop(c * per, (c + 1) * per, prepare, 0)
    for copy in edge:
        copy.wait()

    keep = [jnp.where(d > 0, 1.0, 0.0), jnp.where(d < nd - 1, 1.0, 0.0)]
    keep_row = [jnp.where(t > 0, 1.0, 0.0), jnp.where(t < nt - 1, 1.0, 0.0)]

    def fill_planes(g, carry):
        for side, place in ((0, 0), (1, cells + 1)):
            for j in range(8):
                v = zh[side, rows_at(8 * g), 128 * j : 128 * j + 128].astype(f32)
                fld[place, j, rows_at(8 * g + 8), :] = v * keep[side]
        return carry

    lax.fori_loop(0, 8, fill_planes, 0)

    def fill_rows(z, carry):
        for side, place in ((0, 7), (1, 72)):
            for j in range(8):
                v = rh[side, z, :, 128 * j : 128 * j + 128].astype(f32)
                fld[z + 1, j, place : place + 1, :] = v * keep_row[side]
        return carry

    lax.fori_loop(0, cells, fill_rows, 0)

    a = level_coeffs(tf_ref)
    sgn = jnp.where(flipped, -1, 1)
    sf = jnp.where(flipped, -1.0, 1.0)
    z0 = jnp.where(flipped, cells + 1, 0)
    lx, ly, lz = (0.65 / 0.35 * c for c in LIGHT)
    lz = lz * sf
    order = jnp.where(flipped, nd - 1 - d, d).astype(f32)
    h0 = order * (cells / 256.0) + 0.5 / 256.0
    h1 = h0 + (cells - 1) / 256.0

    def march(j, dst, slot):
        def bands(b, carry):
            base = 8 * BANDS * b

            def cell(k, state):
                zc = z0 + sgn * (k + 1)
                new = []
                for i in range(BANDS):
                    prev, cur, S, T, sums, aw, c1, c2, c3, nx, ny, nz = state[i]
                    r0 = base + 8 * i
                    nxt = fld[zc + sgn, j, rows_at(r0 + 8), :]
                    gx = gxs[zc - 1, j, rows_at(r0), :]
                    gy = fld[zc, j, pl.ds(r0 + 9, 8), :] - fld[zc, j, pl.ds(r0 + 7, 8), :]
                    gz = nxt - prev
                    r = lax.rsqrt((gx * gx + gy * gy) + (gz * gz + 65025.0))
                    S = S + jnp.log2(1.0 + jnp.exp2(poly(a[0], cur)))
                    after = jnp.exp2(S * -0.008)
                    w = T - after
                    sums = sums + T
                    wr = w * r
                    ws = w + wr * jnp.abs(gx * lx + gy * ly + gz * lz)
                    aw = aw + ws
                    c1 = c1 + ws * jnp.tanh(poly(a[1], cur))
                    c2 = c2 + ws * jnp.tanh(poly(a[2], cur))
                    c3 = c3 + ws * jnp.tanh(poly(a[3], cur))
                    nx = nx + wr * gx
                    ny = ny + wr * gy
                    nz = nz + wr * gz
                    new.append((cur, nxt, S, after, sums, aw, c1, c2, c3, nx, ny, nz))
                return tuple(new)

            start = []
            for i in range(BANDS):
                first = fld[z0, j, rows_at(base + 8 * i + 8), :]
                zero = first * 0.0
                start.append((first, fld[z0 + sgn, j, rows_at(base + 8 * i + 8), :], zero, zero + 1.0) + (zero,) * 8)
            done = lax.fori_loop(0, cells, cell, tuple(start), unroll=16)
            for i in range(BANDS):
                _, _, _, T, sums, aw, c1, c2, c3, nx, ny, nz = done[i]
                height = (h0 - 1.0 / 256.0) + sums * (1.0 / 256.0) - T * h1
                planes = (0.175 * (aw + c1), 0.175 * (aw + c2), 0.175 * (aw + c3), T, height, nx, ny, nz * sf)
                for p in range(8):
                    dst[slot, p, rows_at(base + 8 * i), :] = planes[p]
            return carry

        lax.fori_loop(0, 8 // BANDS, bands, 0)

    own_front = core == flip

    def to_sibling(s):
        return remote(outb.at[s], sibr.at[s], ss.at[s], sr.at[s], {"depth": sib})

    def to_chip(s, e):
        return remote(mine.at[s], parts.at[(4 - e) % 4], cs.at[s], cr.at[(4 - e) % 4], {"depth": (d + 2 * e) % nd})

    def offset(s):
        return (10 - s + 3 * (s * (s - 1) // 2)) % 4

    def step(s, carry):
        e = offset(s)
        block = 2 * ((chip + e) % 4)
        march(block + 1 - core, outb, s)
        to_sibling(s).start()
        march(block + core, mine, s)
        to_sibling(s).wait_recv()

        def merge(g, c):
            rows = rows_at(8 * g)
            x = [mine[s, p, rows, :] for p in range(8)]
            y = [sibr[s, p, rows, :] for p in range(8)]
            front = [jnp.where(own_front, x[p], y[p]) for p in range(8)]
            back = [jnp.where(own_front, y[p], x[p]) for p in range(8)]
            for p in range(8):
                mine[s, p, rows, :] = front[3] * back[p] if p == 3 else front[p] + front[3] * back[p]
            return c

        lax.fori_loop(0, 8, merge, 0)

        @pl.when(s < 3)
        def _():
            to_chip(s, e).start()

        return carry

    lax.fori_loop(0, 4, step, 0)
    for s in range(3):
        to_chip(s, (2, 1, 3)[s]).wait_recv()

    kd, kn = (20.0 * LOG2E) ** 0.5, (2.0 * LOG2E) ** 0.5

    def finish(g, carry):
        rows = rows_at(8 * g)

        def part(i):
            who = jnp.where(flipped, 3 - i, i)
            slot = (who - chip + 4) % 4
            inside = slot == 0
            return [jnp.where(inside, mine[3, p, rows, :], parts[slot, p, rows, :]) for p in range(8)]

        acc = part(0)
        for i in range(1, 4):
            back = part(i)
            acc = [acc[3] * back[p] if p == 3 else acc[p] + acc[3] * back[p] for p in range(8)]
        nx, ny, nz = acc[5:8]
        facing = jnp.maximum(LIGHT[0] * nx + LIGHT[1] * ny + LIGHT[2] * nz, 0.0)
        glow = 0.4 + 0.6 * facing
        f = [acc[4] * kd, nx * kn, ny * kn, nz * kn]
        bias = jnp.log2(jnp.maximum(1.0 - acc[3], 1e-37))
        for v in f:
            bias = bias - v * v
        f += [bias] + [acc[p] * glow for p in range(3)]
        packed = pltpu.roll(f[0], 8, 1)
        for p in range(8):
            feat[p, rows_at(8 * g + 8), :] = f[p]
            if p:
                packed = jnp.where(lane >= 16 * p, pltpu.roll(f[p], 16 * p + 8 if p < 7 else 120, 1), packed)
        pk[rows, :] = packed
        return carry

    lax.fori_loop(0, 8, finish, 0)

    top, bottom = pl.ds(0, 8), pl.ds(72, 8)
    halo = [
        remote(feat.at[:, pl.ds(8, 8)], feat.at[:, bottom], hs.at[0], hr.at[0], {"tile": dn_t}),
        remote(feat.at[:, pl.ds(64, 8)], feat.at[:, top], hs.at[1], hr.at[1], {"tile": up_t}),
        remote(pk, he.at[pl.ds(8, 64)], hs.at[2], hr.at[2], {"depth": dn_d}),
        remote(pk, hw.at[pl.ds(8, 64)], hs.at[3], hr.at[3], {"depth": up_d}),
        remote(pk.at[pl.ds(0, 8)], he.at[bottom], hs.at[4], hr.at[4], {"depth": dn_d, "tile": dn_t}),
        remote(pk.at[pl.ds(56, 8)], he.at[top], hs.at[5], hr.at[5], {"depth": dn_d, "tile": up_t}),
        remote(pk.at[pl.ds(0, 8)], hw.at[bottom], hs.at[6], hr.at[6], {"depth": up_d, "tile": dn_t}),
        remote(pk.at[pl.ds(56, 8)], hw.at[top], hs.at[7], hr.at[7], {"depth": up_d, "tile": up_t}),
    ]
    for copy in halo:
        copy.start()
    for copy in halo:
        copy.wait()
    for s in range(4):
        to_sibling(s).wait_send()
    for s in range(3):
        to_chip(s, (2, 1, 3)[s]).wait_send()

    def shift_rows(i, carry):
        rows = rows_at(8 * i)
        both = jnp.where(lane % 16 < 8, hw[rows, :], he[rows, :])
        absent = ((i == 0) & (t == 0)) | ((i == 9) & (t == nt - 1))
        for p in range(8):
            x = feat[p, rows, :]
            h = pltpu.roll(both, (120 - 16 * p) % 128, 1)
            if p == 4:
                outside = jnp.where(lane < 64, jnp.where(d == nd - 1, 1, 0), jnp.where(d == 0, 1, 0))
                h = jnp.where(outside == 1, -1e30, h)
                h = jnp.where(absent, -1e30, h)
                x = jnp.where(absent, -1e30, x)
            for k in range(SPAN):
                dx = k - RADIUS
                if dx == 0:
                    y = x
                elif dx > 0:
                    y = pltpu.roll(jnp.where(lane < dx, h, x), 128 - dx, 1)
                else:
                    y = pltpu.roll(jnp.where(lane >= 128 + dx, h, x), -dx, 1)
                if p == 4:
                    y = y - dx * dx * (LOG2E / 72.0)
                shf[k, p, rows, :] = y
        return carry

    lax.fori_loop(0, 10, shift_rows, 0)

    def shade(g, carry):
        own = [feat[p, rows_at(8 * g + 8), :] for p in range(4)]
        twice = [v * 2.0 for v in own]
        zero = own[0] * 0.0

        def line(dy, sums):
            rows = pl.ds(8 * g + dy, 8)
            part = [None] * 4
            for k in range(SPAN):
                e = shf[k, 4, rows, :]
                for p in range(4):
                    e = e + twice[p] * shf[k, p, rows, :]
                w = jnp.exp2(e)
                for c in range(3):
                    term = w * shf[k, 5 + c, rows, :]
                    part[c] = term if k == 0 else part[c] + term
                part[3] = w if k == 0 else part[3] + w
            rise = (dy - RADIUS).astype(f32)
            fall = jnp.exp2(zero + rise * rise * (-LOG2E / 72.0))
            return tuple(sums[c] + fall * part[c] for c in range(4))

        sums = lax.fori_loop(0, SPAN, line, (zero,) * 4)
        norm = own[0] * own[0]
        for v in own[1:]:
            norm = norm + v * v
        scale = jnp.exp2(-norm)
        inv = scale / (1.0 + scale * sums[3])
        for c in range(3):
            out_ref[c, rows_at(8 * g), :] = sums[c] * inv
        return carry

    lax.fori_loop(0, 8, shade, 0)


def per_device(density, view_flip, tf_coeff):
    i32 = jnp.int32
    dma = pltpu.SemaphoreType.DMA
    image = (8, 64, 128)
    return pl.pallas_call(
        kernel,
        out_shape=jax.ShapeDtypeStruct((3, 64, 128), f32),
        in_specs=[
            pl.BlockSpec(memory_space=pltpu.SMEM),
            pl.BlockSpec(memory_space=pltpu.SMEM),
            pl.BlockSpec(memory_space=pl.ANY),
        ],
        out_specs=pl.BlockSpec(memory_space=pltpu.VMEM),
        scratch_shapes=[
            pltpu.VMEM((32, 64, 1024), i32),
            pltpu.VMEM((34, 8, 80, 128), f32),
            pltpu.VMEM((32, 8, 64, 128), f32),
            pltpu.VMEM((2, 64, 1024), i32),
            pltpu.VMEM((2, 32, 1, 1024), i32),
            pltpu.VMEM((4,) + image, f32),
            pltpu.VMEM((4,) + image, f32),
            pltpu.VMEM((4,) + image, f32),
            pltpu.VMEM((4,) + image, f32),
            pltpu.VMEM((8, 80, 128), f32),
            pltpu.VMEM((64, 128), f32),
            pltpu.VMEM((80, 128), f32),
            pltpu.VMEM((80, 128), f32),
            pltpu.VMEM((SPAN, 8, 80, 128), f32),
            dma((CHUNKS,)),
            dma((2,)), dma((2,)),
            dma((2,)), dma((2,)),
            dma((4,)), dma((4,)),
            dma((4,)), dma((4,)),
            dma((8,)), dma((8,)),
        ],
        compiler_params=pltpu.CompilerParams(
            collective_id=0, has_side_effects=True, vmem_limit_bytes=60 * 1024 * 1024
        ),
        name="render",
    )(view_flip, tf_coeff, density)


def solution(mesh):
    in_specs = (P("depth", "tile", None), P("tile"), P())
    out_specs = P(None, "tile", "depth")
    return jax.shard_map(per_device, mesh=mesh, in_specs=in_specs, out_specs=out_specs, check_vma=False)
```

time: 228 us -> 60.9 us (0.27)
  the two profiles are of different devices: /device:TPU:15 before, /device:TPU:1 now
where the time goes in v1:
time: 60.9 us; the launch traced here: 60.8 us
  Pallas kernels  58.6 us (96%)
  local copies, waits for them, and re-layouts  1.54 us (3%)
  between operations  0.66 us (1%)
    pallas_call x1, Pallas kernels, per_device(): pl.pallas_call(kernel, out_shape=jax.ShapeDtypeStruct((3, 64, 128), f32),...  58.6 us
    unnamed x1, local copies, waits for them, and re-layouts  1.54 us

profile of v1, /device:TPU:1, one launch (start us, length us, event | category | flops | bytes accessed | tf_op | source)
XLA Modules:
  0.0 60.8 jit_solution(2914885066479202519)
XLA Ops:
  0.7 58.6 %render.1 = f32[3,64,128]{2,1,0:T(8,128)} custom-call(s32[1]{0:T(128)S(6)} %copy.5.flip_ref, f32[4,4]{1,0:T(4,128)} %tf_ref.1, s32[32,64,1024]{2,1,0:T(8,128)} %dens.1), custom_call_target="tpu_custom_call" | custom-call | tf_op jit(solution)/shard_map/render/pallas_call | solution.py:340
  59.2 1.5 %copy.6 = f32[3,64,128]{2,1,0:T(8,128)} copy(f32[3,64,128]{2,1,0:T(8,128)} %render.1) | data formatting | bytes 196608

commit v2 on v1

v2 whole, which is shorter than its diff:
```python
import jax
import jax.numpy as jnp
from jax import lax
from jax.experimental import pallas as pl
from jax.experimental.pallas import tpu as pltpu
from jax.sharding import PartitionSpec as P

f32 = jnp.float32
LOG2E = 1.4426950408889634
LIGHT = (0.48, 0.6, 0.64)
RADIUS = 8
SPAN = 2 * RADIUS + 1
BANDS = 2


def rows_at(start, count=8):
    return pl.ds(pl.multiple_of(start, 8), count)


def poly(a, x):
    return a[0] + x * (a[1] + x * (a[2] + x * a[3]))


def level_coeffs(tf):
    s = 2.0 / 255.0
    table = []
    for q in range(4):
        c0, c1, c2, c3 = (tf[q, i] for i in range(4))
        m = LOG2E if q == 0 else 0.5
        table.append(
            (
                (c0 - c1 + c2 - c3) * m,
                (c1 - 2.0 * c2 + 3.0 * c3) * (s * m),
                (c2 - 3.0 * c3) * (s * s * m),
                c3 * (s * s * s * m),
            )
        )
    return table


def kernel(flip_ref, tf_ref, dens, out_ref, raw, fld, zh, rh, inner, image, sibr, parts, feat, pk, hw, he, rim, shf, tot,
           load_sem, zs, zr, rs, rr, ss, sr, cs, cr, hs, hr):
    nd, nt = 8, 32
    d, t = lax.axis_index("depth"), lax.axis_index("tile")
    core, chip = d % 2, d // 2
    flip = flip_ref[0]
    flipped = flip == 1
    cells = dens.shape[0]
    up_d, dn_d = (d + 1) % nd, (d + nd - 1) % nd
    up_t, dn_t = (t + 1) % nt, (t + nt - 1) % nt
    sib = 2 * chip + 1 - core

    def load(i):
        j = (2 * ((chip + 2) % 4) + 7 + i) % 8
        piece = dens.at[:, :, pl.ds(pl.multiple_of(128 * j, 128), 128)]
        return j, pltpu.make_async_copy(piece, raw.at[j], load_sem.at[i])

    for i in range(8):
        load(i)[1].start()

    barrier = pltpu.get_barrier_semaphore()
    near = [{"depth": up_d}, {"depth": dn_d}, {"tile": up_t}, {"tile": dn_t}]
    near += [{"depth": a, "tile": b} for a in (up_d, dn_d) for b in (up_t, dn_t)]
    near += [{"depth": (d + 2 * e) % nd} for e in (1, 2, 3)]
    for who in near:
        pl.semaphore_signal(barrier, inc=1, device_id=who, device_id_type=pl.DeviceIdType.MESH)

    def clear(z, carry):
        for j in (0, 9):
            for g in range(8):
                fld[z + 1, j, 8 * g + 8 : 8 * g + 16, :] = jnp.zeros((8, 128), f32)
        return carry

    lax.fori_loop(0, cells, clear, 0)
    pl.semaphore_wait(barrier, len(near))

    def remote(src, dst, send, recv, who):
        return pltpu.make_async_remote_copy(src_ref=src, dst_ref=dst, send_sem=send, recv_sem=recv, device_id=who,
                                            device_id_type=pl.DeviceIdType.MESH)

    edge = [
        remote(dens.at[cells - 1], zh.at[0], zs.at[0], zr.at[0], {"depth": up_d}),
        remote(dens.at[0], zh.at[1], zs.at[1], zr.at[1], {"depth": dn_d}),
        remote(dens.at[:, pl.ds(63, 1)], rh.at[0], rs.at[0], rr.at[0], {"tile": up_t}),
        remote(dens.at[:, pl.ds(0, 1)], rh.at[1], rs.at[1], rr.at[1], {"tile": dn_t}),
    ]
    for copy in edge:
        copy.start()

    lane = lax.broadcasted_iota(jnp.int32, (8, 128), 1)
    first_lane, last_lane = lane == 0, lane == 127
    a = level_coeffs(tf_ref)
    sgn = jnp.where(flipped, -1, 1)
    sf = jnp.where(flipped, -1.0, 1.0)
    z0 = jnp.where(flipped, cells + 1, 0)
    lx, ly, lz = (0.65 / 0.35 * c for c in LIGHT)
    lz = lz * sf
    order = jnp.where(flipped, nd - 1 - d, d).astype(f32)
    h0 = order * (cells / 256.0) + 0.5 / 256.0
    h1 = h0 + (cells - 1) / 256.0

    def place(b, i):
        return 8 * ((BANDS * b + 1 + i) % 8)

    def cell(j, b):
        def body(k, state):
            zc = z0 + sgn * (k + 1)
            new = []
            for i in range(BANDS):
                prev, cur, S, T, sums, aw, c1, c2, c3, nx, ny, nz = state[i]
                r0 = place(b, i)
                rows = rows_at(r0 + 8)
                nxt = fld[zc + sgn, j, rows, :]
                right, left = fld[zc, j + 1, rows, :], fld[zc, j - 1, rows, :]
                ahead = pltpu.roll(jnp.where(first_lane, right, cur), 127, 1)
                behind = pltpu.roll(jnp.where(last_lane, left, cur), 1, 1)
                gx = ahead - behind
                gy = fld[zc, j, pl.ds(r0 + 9, 8), :] - fld[zc, j, pl.ds(r0 + 7, 8), :]
                gz = nxt - prev
                r = lax.rsqrt((gx * gx + gy * gy) + (gz * gz + 65025.0))
                S = S + jnp.log2(1.0 + jnp.exp2(poly(a[0], cur)))
                after = jnp.exp2(S * -0.008)
                w = T - after
                sums = sums + T
                wr = w * r
                ws = w + wr * jnp.abs(gx * lx + gy * ly + gz * lz)
                aw = aw + ws
                c1 = c1 + ws * jnp.tanh(poly(a[1], cur))
                c2 = c2 + ws * jnp.tanh(poly(a[2], cur))
                c3 = c3 + ws * jnp.tanh(poly(a[3], cur))
                nx = nx + wr * gx
                ny = ny + wr * gy
                nz = nz + wr * gz
                new.append((cur, nxt, S, after, sums, aw, c1, c2, c3, nx, ny, nz))
            return tuple(new)

        return body

    def enter(j, b, k):
        start = []
        for i in range(BANDS):
            rows = rows_at(place(b, i) + 8)
            prev, cur = fld[z0 + sgn * k, j, rows, :], fld[z0 + sgn * (k + 1), j, rows, :]
            zero = cur * 0.0
            start.append((prev, cur, zero, zero + 1.0) + (zero,) * 8)
        return tuple(start)

    def leave(state, b, slot):
        for i in range(BANDS):
            _, _, _, T, sums, aw, c1, c2, c3, nx, ny, nz = state[i]
            height = (h0 - 1.0 / 256.0) + sums * (1.0 / 256.0) - T * h1
            planes = (0.175 * (aw + c1), 0.175 * (aw + c2), 0.175 * (aw + c3), T, height, nx, ny, nz * sf)
            for p in range(8):
                image[slot, p, rows_at(place(b, i)), :] = planes[p]

    def offset(s):
        return (10 - s + 3 * (s * (s - 1) // 2)) % 4

    def block_of(h):
        return 2 * ((chip + offset(h // 2)) % 4) + (h + core + 1) % 2 + 1

    def take(i, carry):
        j, copy = load(i)
        copy.wait()

        def layer(z, c):
            for g in range(8):
                fld[z + 1, j + 1, 8 * g + 8 : 8 * g + 16, :] = raw[j, z, 8 * g : 8 * g + 8, :].astype(f32)
            return c

        return lax.fori_loop(0, cells, layer, carry, unroll=2)

    lax.fori_loop(0, 4, take, 0)

    def early(n, carry):
        h, b = n // 3, n % 3
        j = block_of(h)
        done = lax.fori_loop(1, cells - 1, cell(j, b), enter(j, b, 1), unroll=15)
        for i in range(BANDS):
            for q, v in enumerate(done[i][2:3] + done[i][4:]):
                inner[h, q, rows_at(place(b, i)), :] = v
        return carry

    lax.fori_loop(0, 6, early, 0)
    lax.fori_loop(4, 8, take, 0)
    for copy in edge:
        copy.wait()

    keep = [jnp.where(d > 0, 1.0, 0.0), jnp.where(d < nd - 1, 1.0, 0.0)]
    keep_row = [jnp.where(t > 0, 1.0, 0.0), jnp.where(t < nt - 1, 1.0, 0.0)]

    def fill_planes(g, carry):
        for side, layer in ((0, 0), (1, cells + 1)):
            for j in range(8):
                v = zh[side, rows_at(8 * g), 128 * j : 128 * j + 128].astype(f32)
                fld[layer, j + 1, rows_at(8 * g + 8), :] = v * keep[side]
        return carry

    lax.fori_loop(0, 8, fill_planes, 0)

    def fill_rows(z, carry):
        for side, row in ((0, 7), (1, 72)):
            for j in range(8):
                v = rh[side, z, :, 128 * j : 128 * j + 128].astype(f32)
                fld[z + 1, j + 1, row : row + 1, :] = v * keep_row[side]
        return carry

    lax.fori_loop(0, cells, fill_rows, 0)

    own_front = core == flip

    def to_sibling(s):
        return remote(image.at[2 * s], sibr.at[s], ss.at[s], sr.at[s], {"depth": sib})

    def to_chip(s, e):
        return remote(image.at[2 * s + 1], parts.at[(4 - e) % 4], cs.at[s], cr.at[(4 - e) % 4],
                      {"depth": (d + 2 * e) % nd})

    def half_step(h, carry):
        j = block_of(h)
        s = h // 2

        def bands(b, c):
            resumed = (h < 2) & (b < 3)

            @pl.when(resumed)
            def _():
                body = cell(j, b)
                state = body(0, enter(j, b, 0))
                mixed = []
                for i in range(BANDS):
                    _, _, S, T, *sums = state[i]
                    rows = rows_at(place(b, i))
                    mid = [inner[h, q, rows, :] for q in range(9)]
                    S = S + mid[0]
                    sums = [v + T * m for v, m in zip(sums, mid[1:])]
                    tail = rows_at(place(b, i) + 8)
                    prev, cur = fld[z0 + sgn * (cells - 1), j, tail, :], fld[z0 + sgn * cells, j, tail, :]
                    mixed.append((prev, cur, S, jnp.exp2(S * -0.008), *sums))
                leave(body(cells - 1, tuple(mixed)), b, h)

            @pl.when(jnp.logical_not(resumed))
            def _():
                leave(lax.fori_loop(0, cells, cell(j, b), enter(j, b, 0), unroll=16), b, h)

            return c

        lax.fori_loop(0, 8 // BANDS, bands, 0)

        @pl.when(h % 2 == 0)
        def _():
            to_sibling(s).start()

        @pl.when(h % 2 == 1)
        def _():
            to_sibling(s).wait_recv()

            def merge(g, c):
                rows = rows_at(8 * g)
                x = [image[h, p, rows, :] for p in range(8)]
                y = [sibr[s, p, rows, :] for p in range(8)]
                front = [jnp.where(own_front, x[p], y[p]) for p in range(8)]
                back = [jnp.where(own_front, y[p], x[p]) for p in range(8)]
                for p in range(8):
                    image[h, p, rows, :] = front[3] * back[p] if p == 3 else front[p] + front[3] * back[p]
                return c

            lax.fori_loop(0, 8, merge, 0)

            @pl.when(s < 3)
            def _():
                to_chip(s, offset(s)).start()

        return carry

    lax.fori_loop(0, 8, half_step, 0)
    for s in range(3):
        to_chip(s, (2, 1, 3)[s]).wait_recv()

    kd, kn = (20.0 * LOG2E) ** 0.5, (2.0 * LOG2E) ** 0.5

    def finish(g, carry):
        rows = rows_at(8 * g)

        def part(i):
            who = jnp.where(flipped, 3 - i, i)
            slot = (who - chip + 4) % 4
            inside = slot == 0
            return [jnp.where(inside, image[7, p, rows, :], parts[slot, p, rows, :]) for p in range(8)]

        acc = part(0)
        for i in range(1, 4):
            back = part(i)
            acc = [acc[3] * back[p] if p == 3 else acc[p] + acc[3] * back[p] for p in range(8)]
        nx, ny, nz = acc[5:8]
        facing = jnp.maximum(LIGHT[0] * nx + LIGHT[1] * ny + LIGHT[2] * nz, 0.0)
        glow = 0.4 + 0.6 * facing
        f = [acc[4] * kd, nx * kn, ny * kn, nz * kn]
        bias = jnp.log2(jnp.maximum(1.0 - acc[3], 1e-37))
        for v in f:
            bias = bias - v * v
        f += [bias] + [acc[p] * glow for p in range(3)]
        packed = pltpu.roll(f[0], 8, 1)
        for p in range(8):
            feat[p, rows_at(8 * g + 8), :] = f[p]
            if p:
                packed = jnp.where(lane >= 16 * p, pltpu.roll(f[p], 16 * p + 8, 1), packed)
        pk[rows, :] = packed
        return carry

    lax.fori_loop(0, 8, finish, 0)

    top, bottom = pl.ds(0, 8), pl.ds(72, 8)
    halo = [
        remote(feat.at[:, pl.ds(8, 8)], feat.at[:, bottom], hs.at[0], hr.at[0], {"tile": dn_t}),
        remote(feat.at[:, pl.ds(64, 8)], feat.at[:, top], hs.at[1], hr.at[1], {"tile": up_t}),
        remote(pk, he.at[pl.ds(8, 64)], hs.at[2], hr.at[2], {"depth": dn_d}),
        remote(pk, hw.at[pl.ds(8, 64)], hs.at[3], hr.at[3], {"depth": up_d}),
        remote(pk.at[pl.ds(0, 8)], he.at[bottom], hs.at[4], hr.at[4], {"depth": dn_d, "tile": dn_t}),
        remote(pk.at[pl.ds(56, 8)], he.at[top], hs.at[5], hr.at[5], {"depth": dn_d, "tile": up_t}),
        remote(pk.at[pl.ds(0, 8)], hw.at[bottom], hs.at[6], hr.at[6], {"depth": up_d, "tile": dn_t}),
        remote(pk.at[pl.ds(56, 8)], hw.at[top], hs.at[7], hr.at[7], {"depth": up_d, "tile": up_t}),
    ]
    for copy in halo:
        copy.start()

    def shift_rows(i, carry):
        rows = rows_at(8 * i)
        for p in range(8):
            x = feat[p, rows, :]
            for k in range(SPAN):
                dx = k - RADIUS
                y = pltpu.roll(x, (-dx) % 128, 1) if dx else x
                if p == 4:
                    y = y - dx * dx * (LOG2E / 72.0)
                    if dx:
                        y = jnp.where(lane >= 128 - dx if dx > 0 else lane < -dx, -1e30, y)
                shf[k, p, rows, :] = y
        return carry

    def fall(dy, like):
        rise = (dy - RADIUS).astype(f32)
        return jnp.exp2(like * 0.0 + rise * rise * (-LOG2E / 72.0))

    def add_tap(part, q, twice):
        e = q[4]
        for p in range(4):
            e = e + twice[p] * q[p]
        w = jnp.exp2(e)
        terms = [w * q[5], w * q[6], w * q[7], w]
        return terms if part is None else [u + v for u, v in zip(part, terms)]

    def inside(g, carry):
        twice = [feat[p, rows_at(8 * g + 8), :] * 2.0 for p in range(4)]

        def line(dy, sums):
            rows = pl.ds(8 * g + dy, 8)
            part = None
            for k in range(SPAN):
                part = add_tap(part, [shf[k, p, rows, :] for p in range(8)], twice)
            f = fall(dy, twice[0])
            return tuple(u + f * v for u, v in zip(sums, part))

        sums = lax.fori_loop(0, SPAN, line, (twice[0] * 0.0,) * 4, unroll=4)
        for c in range(4):
            tot[c, rows_at(8 * g), :] = sums[c]
        return carry

    lax.fori_loop(1, 9, shift_rows, 0)
    lax.fori_loop(1, 7, inside, 0)
    for copy in halo:
        copy.wait()

    def absent(i):
        return ((i == 0) & (t == 0)) | ((i == 9) & (t == nt - 1))

    def outer_rows(n, carry):
        i = 9 * n
        rows = rows_at(8 * i)
        feat[4, rows, :] = jnp.where(absent(i), -1e30, feat[4, rows, :])
        shift_rows(i, 0)
        return inside(7 * n, carry)

    lax.fori_loop(0, 2, outer_rows, 0)

    e, m = lane // 8, lane % 8
    left = e < 8
    column = e + m
    there = jnp.where(left, jnp.where(column <= 7, 1, 0), jnp.where(column >= 15, 1, 0))
    there = there * jnp.where(left, jnp.where(d > 0, 1, 0), jnp.where(d < nd - 1, 1, 0))
    source = jnp.where(left, column % 8, 8 + (column + 1) % 8)
    run = jnp.where(left, 8 - m, m + 1).astype(f32)
    drop = jnp.where(there == 1, run * run * (-LOG2E / 72.0), -1e30)
    pixel = jnp.where(left, e, 112 + e)
    home = jnp.where(lane < 8, 8 * lane, jnp.where(lane >= 120, 8 * (lane - 112), 0))
    edge_lane = (lane < 8) | (lane >= 120)

    def rim_rows(i, carry):
        rows = rows_at(8 * i)
        both = jnp.where(lane % 16 < 8, hw[rows, :], he[rows, :])
        for p in range(8):
            v = jnp.take_along_axis(both, source + 16 * p, axis=1)
            if p == 4:
                v = jnp.where(absent(i), -1e30, v + drop)
            rim[p, rows, :] = v
        return carry

    lax.fori_loop(0, 10, rim_rows, 0)

    def outside(g, carry):
        own = [feat[p, rows_at(8 * g + 8), :] for p in range(4)]
        twice = [jnp.take_along_axis(v * 2.0, pixel, axis=1) for v in own]

        def line(dy, sums):
            part = add_tap(None, [rim[p, pl.ds(8 * g + dy, 8), :] for p in range(8)], twice)
            f = fall(dy, twice[0])
            return tuple(u + f * v for u, v in zip(sums, part))

        sums = lax.fori_loop(0, SPAN, line, (twice[0] * 0.0,) * 4, unroll=17)
        total = []
        for c in range(4):
            v = sums[c]
            for step in (1, 2, 4):
                v = v + pltpu.roll(v, 128 - step, 1)
            v = jnp.take_along_axis(v, home, axis=1)
            total.append(tot[c, rows_at(8 * g), :] + jnp.where(edge_lane, v, 0.0))
        norm = own[0] * own[0]
        for v in own[1:]:
            norm = norm + v * v
        scale = jnp.exp2(-norm)
        inv = scale / (1.0 + scale * total[3])
        for c in range(3):
            out_ref[c, rows_at(8 * g), :] = total[c] * inv
        return carry

    lax.fori_loop(0, 8, outside, 0)
    for s in range(4):
        to_sibling(s).wait_send()
    for s in range(3):
        to_chip(s, (2, 1, 3)[s]).wait_send()


def per_device(density, view_flip, tf_coeff):
    i32 = jnp.int32
    dma = pltpu.SemaphoreType.DMA
    image = (8, 64, 128)
    return pl.pallas_call(
        kernel,
        out_shape=jax.ShapeDtypeStruct((3, 64, 128), f32),
        in_specs=[
            pl.BlockSpec(memory_space=pltpu.SMEM),
            pl.BlockSpec(memory_space=pltpu.SMEM),
            pl.BlockSpec(memory_space=pl.ANY),
        ],
        out_specs=pl.BlockSpec(memory_space=pltpu.VMEM),
        scratch_shapes=[
            pltpu.VMEM((8, 32, 64, 128), i32),
            pltpu.VMEM((34, 10, 80, 128), f32),
            pltpu.VMEM((2, 64, 1024), i32),
            pltpu.VMEM((2, 32, 1, 1024), i32),
            pltpu.VMEM((2, 9, 64, 128), f32),
            pltpu.VMEM((8,) + image, f32),
            pltpu.VMEM((4,) + image, f32),
            pltpu.VMEM((4,) + image, f32),
            pltpu.VMEM((8, 80, 128), f32),
            pltpu.VMEM((64, 128), f32),
            pltpu.VMEM((80, 128), f32),
            pltpu.VMEM((80, 128), f32),
            pltpu.VMEM((8, 80, 128), f32),
            pltpu.VMEM((SPAN, 8, 80, 128), f32),
            pltpu.VMEM((4, 64, 128), f32),
            dma((8,)),
            dma((2,)), dma((2,)),
            dma((2,)), dma((2,)),
            dma((4,)), dma((4,)),
            dma((4,)), dma((4,)),
            dma((8,)), dma((8,)),
        ],
        compiler_params=pltpu.CompilerParams(
            collective_id=0, has_side_effects=True, vmem_limit_bytes=60 * 1024 * 1024
        ),
        name="render",
    )(view_flip, tf_coeff, density)


def solution(mesh):
    in_specs = (P("depth", "tile", None), P("tile"), P())
    out_specs = P(None, "tile", "depth")
    return jax.shard_map(per_device, mesh=mesh, in_specs=in_specs, out_specs=out_specs, check_vma=False)
```

time: 60.9 us -> 55.7 us (0.915)
  Pallas kernels: 58.6 us -> 53.4 us
    pallas_call x1, Pallas kernels: 58.6 us -> 53.4 us  [per_device(): pl.pallas_call(kernel, out_shape=jax.ShapeDtypeStruct((3, 64, 128), f32),...]
where the time goes in v2:
time: 55.7 us; the launch traced here: 55.6 us
  Pallas kernels  53.4 us (96%)
  local copies, waits for them, and re-layouts  1.54 us (3%)
  between operations  0.66 us (1%)
    pallas_call x1, Pallas kernels, per_device(): pl.pallas_call(kernel, out_shape=jax.ShapeDtypeStruct((3, 64, 128), f32),...  53.4 us
    unnamed x1, local copies, waits for them, and re-layouts  1.54 us

profile of v2, /device:TPU:1, one launch (start us, length us, event | category | flops | bytes accessed | tf_op | source)
XLA Modules:
  0.0 55.6 jit_solution(11367481201282954585)
XLA Ops:
  0.7 53.4 %render.1 = f32[3,64,128]{2,1,0:T(8,128)} custom-call(s32[1]{0:T(128)S(6)} %copy.5.flip_ref, f32[4,4]{1,0:T(4,128)} %tf_ref.1, s32[32,64,1024]{2,1,0:T(8,128)} %dens.1), custom_call_target="tpu_custom_call" | custom-call | tf_op jit(solution)/shard_map/render/pallas_call | solution.py:447
  54.0 1.5 %copy.6 = f32[3,64,128]{2,1,0:T(8,128)} copy(f32[3,64,128]{2,1,0:T(8,128)} %render.1) | data formatting | bytes 196608

commit v3 on v2

--- a/solution.py
+++ b/solution.py
@@ -107,7 +107,7 @@
             zc = z0 + sgn * (k + 1)
             new = []
             for i in range(BANDS):
-                prev, cur, S, T, sums, aw, c1, c2, c3, nx, ny, nz = state[i]
+                prev, cur, S, T, sums, aw, c1, c2, c3, nx, ny, nl = state[i]
                 r0 = place(b, i)
                 rows = rows_at(r0 + 8)
                 nxt = fld[zc + sgn, j, rows, :]
@@ -123,15 +123,16 @@
                 w = T - after
                 sums = sums + T
                 wr = w * r
-                ws = w + wr * jnp.abs(gx * lx + gy * ly + gz * lz)
+                lit = wr * (gx * lx + gy * ly + gz * lz)
+                ws = w + jnp.abs(lit)
                 aw = aw + ws
                 c1 = c1 + ws * jnp.tanh(poly(a[1], cur))
                 c2 = c2 + ws * jnp.tanh(poly(a[2], cur))
                 c3 = c3 + ws * jnp.tanh(poly(a[3], cur))
                 nx = nx + wr * gx
                 ny = ny + wr * gy
-                nz = nz + wr * gz
-                new.append((cur, nxt, S, after, sums, aw, c1, c2, c3, nx, ny, nz))
+                nl = nl + lit
+                new.append((cur, nxt, S, after, sums, aw, c1, c2, c3, nx, ny, nl))
             return tuple(new)
 
         return body
@@ -147,9 +148,10 @@
 
     def leave(state, b, slot):
         for i in range(BANDS):
-            _, _, _, T, sums, aw, c1, c2, c3, nx, ny, nz = state[i]
+            _, _, _, T, sums, aw, c1, c2, c3, nx, ny, nl = state[i]
+            nz = (nl - lx * nx - ly * ny) * (0.35 / 0.65 / LIGHT[2])
             height = (h0 - 1.0 / 256.0) + sums * (1.0 / 256.0) - T * h1
-            planes = (0.175 * (aw + c1), 0.175 * (aw + c2), 0.175 * (aw + c3), T, height, nx, ny, nz * sf)
+            planes = (0.175 * (aw + c1), 0.175 * (aw + c2), 0.175 * (aw + c3), T, height, nx, ny, nz)
             for p in range(8):
                 image[slot, p, rows_at(place(b, i)), :] = planes[p]
 
@@ -175,7 +177,7 @@
     def early(n, carry):
         h, b = n // 3, n % 3
         j = block_of(h)
-        done = lax.fori_loop(1, cells - 1, cell(j, b), enter(j, b, 1), unroll=15)
+        done = lax.fori_loop(1, cells - 1, cell(j, b), enter(j, b, 1), unroll=30)
         for i in range(BANDS):
             for q, v in enumerate(done[i][2:3] + done[i][4:]):
                 inner[h, q, rows_at(place(b, i)), :] = v
@@ -205,7 +207,7 @@
                 fld[z + 1, j + 1, row : row + 1, :] = v * keep_row[side]
         return carry
 
-    lax.fori_loop(0, cells, fill_rows, 0)
+    lax.fori_loop(0, cells, fill_rows, 0, unroll=2)
 
     own_front = core == flip
 
@@ -241,7 +243,7 @@
 
             @pl.when(jnp.logical_not(resumed))
             def _():
-                leave(lax.fori_loop(0, cells, cell(j, b), enter(j, b, 0), unroll=16), b, h)
+                leave(lax.fori_loop(0, cells, cell(j, b), enter(j, b, 0), unroll=32), b, h)
 
             return c
 
@@ -265,7 +267,7 @@
                     image[h, p, rows, :] = front[3] * back[p] if p == 3 else front[p] + front[3] * back[p]
                 return c
 
-            lax.fori_loop(0, 8, merge, 0)
+            lax.fori_loop(0, 8, merge, 0, unroll=2)
 
             @pl.when(s < 3)
             def _():
@@ -308,7 +310,7 @@
         pk[rows, :] = packed
         return carry
 
-    lax.fori_loop(0, 8, finish, 0)
+    lax.fori_loop(0, 8, finish, 0, unroll=2)
 
     top, bottom = pl.ds(0, 8), pl.ds(72, 8)
     halo = [
@@ -366,7 +368,7 @@
             tot[c, rows_at(8 * g), :] = sums[c]
         return carry
 
-    lax.fori_loop(1, 9, shift_rows, 0)
+    lax.fori_loop(1, 9, shift_rows, 0, unroll=2)
     lax.fori_loop(1, 7, inside, 0)
     for copy in halo:
         copy.wait()
@@ -383,12 +385,12 @@
 
     lax.fori_loop(0, 2, outer_rows, 0)
 
-    e, m = lane // 8, lane % 8
+    e, m = lane >> 3, lane & 7
     left = e < 8
     column = e + m
     there = jnp.where(left, jnp.where(column <= 7, 1, 0), jnp.where(column >= 15, 1, 0))
     there = there * jnp.where(left, jnp.where(d > 0, 1, 0), jnp.where(d < nd - 1, 1, 0))
-    source = jnp.where(left, column % 8, 8 + (column + 1) % 8)
+    source = jnp.where(left, column & 7, 8 + ((column + 1) & 7))
     run = jnp.where(left, 8 - m, m + 1).astype(f32)
     drop = jnp.where(there == 1, run * run * (-LOG2E / 72.0), -1e30)
     pixel = jnp.where(left, e, 112 + e)
@@ -397,7 +399,7 @@
 
     def rim_rows(i, carry):
         rows = rows_at(8 * i)
-        both = jnp.where(lane % 16 < 8, hw[rows, :], he[rows, :])
+        both = jnp.where((lane & 15) < 8, hw[rows, :], he[rows, :])
         for p in range(8):
             v = jnp.take_along_axis(both, source + 16 * p, axis=1)
             if p == 4:
@@ -405,35 +407,41 @@
             rim[p, rows, :] = v
         return carry
 
-    lax.fori_loop(0, 10, rim_rows, 0)
-
-    def outside(g, carry):
-        own = [feat[p, rows_at(8 * g + 8), :] for p in range(4)]
-        twice = [jnp.take_along_axis(v * 2.0, pixel, axis=1) for v in own]
+    lax.fori_loop(0, 10, rim_rows, 0, unroll=5)
+
+    def outside(G, carry):
+        groups = [4 * G + i for i in range(4)]
+        own = [[feat[p, rows_at(8 * g + 8), :] for p in range(4)] for g in groups]
+        twice = [[jnp.take_along_axis(v * 2.0, pixel, axis=1) for v in o] for o in own]
+        scale = []
+        for o in own:
+            norm = o[0] * o[0]
+            for v in o[1:]:
+                norm = norm + v * v
+            scale.append(jnp.exp2(-norm))
 
         def line(dy, sums):
-            part = add_tap(None, [rim[p, pl.ds(8 * g + dy, 8), :] for p in range(8)], twice)
-            f = fall(dy, twice[0])
-            return tuple(u + f * v for u, v in zip(sums, part))
-
-        sums = lax.fori_loop(0, SPAN, line, (twice[0] * 0.0,) * 4, unroll=17)
-        total = []
-        for c in range(4):
-            v = sums[c]
-            for step in (1, 2, 4):
-                v = v + pltpu.roll(v, 128 - step, 1)
-            v = jnp.take_along_axis(v, home, axis=1)
-            total.append(tot[c, rows_at(8 * g), :] + jnp.where(edge_lane, v, 0.0))
-        norm = own[0] * own[0]
-        for v in own[1:]:
-            norm = norm + v * v
-        scale = jnp.exp2(-norm)
-        inv = scale / (1.0 + scale * total[3])
-        for c in range(3):
-            out_ref[c, rows_at(8 * g), :] = total[c] * inv
-        return carry
-
-    lax.fori_loop(0, 8, outside, 0)
+            f = fall(dy, twice[0][0])
+            new = []
+            for g, tw, sm in zip(groups, twice, sums):
+                part = add_tap(None, [rim[p, pl.ds(8 * g + dy, 8), :] for p in range(8)], tw)
+                new.append(tuple(u + f * v for u, v in zip(sm, part)))
+            return tuple(new)
+
+        sums = lax.fori_loop(0, SPAN, line, ((twice[0][0] * 0.0,) * 4,) * 4, unroll=17)
+        flat = [v for sm in sums for v in sm]
+        for step in (1, 2, 4):
+            turned = [pltpu.roll(v, 128 - step, 1) for v in flat]
+            flat = [v + u for v, u in zip(flat, turned)]
+        flat = [jnp.take_along_axis(v, home, axis=1) for v in flat]
+        for i, g in enumerate(groups):
+            total = [tot[c, rows_at(8 * g), :] + jnp.where(edge_lane, flat[4 * i + c], 0.0) for c in range(4)]
+            inv = scale[i] / (1.0 + scale[i] * total[3])
+            for c in range(3):
+                out_ref[c, rows_at(8 * g), :] = total[c] * inv
+        return carry
+
+    lax.fori_loop(0, 2, outside, 0)
     for s in range(4):
         to_sibling(s).wait_send()
     for s in range(3):

time: 55.7 us -> 51.7 us (0.928)
  Pallas kernels: 53.4 us -> 49.3 us
    pallas_call x1, Pallas kernels: 53.4 us -> 49.3 us  [per_device(): pl.pallas_call(kernel, out_shape=jax.ShapeDtypeStruct((3, 64, 128), f32),...]
where the time goes in v3:
time: 51.7 us; the launch traced here: 51.5 us
  Pallas kernels  49.3 us (95%)
  local copies, waits for them, and re-layouts  1.54 us (3%)
  between operations  0.66 us (1%)
    pallas_call x1, Pallas kernels, per_device(): pl.pallas_call(kernel, out_shape=jax.ShapeDtypeStruct((3, 64, 128), f32),...  49.3 us
    unnamed x1, local copies, waits for them, and re-layouts  1.54 us

profile of v3, /device:TPU:1, one launch (start us, length us, event | category | flops | bytes accessed | tf_op | source)
XLA Modules:
  0.0 51.5 jit_solution(12719217763682010109)
XLA Ops:
  0.7 49.3 %render.1 = f32[3,64,128]{2,1,0:T(8,128)} custom-call(s32[1]{0:T(128)S(6)} %copy.5.flip_ref, f32[4,4]{1,0:T(4,128)} %tf_ref.1, s32[32,64,1024]{2,1,0:T(8,128)} %dens.1), custom_call_target="tpu_custom_call" | custom-call | tf_op jit(solution)/shard_map/render/pallas_call | solution.py:455
  50.0 1.5 %copy.6 = f32[3,64,128]{2,1,0:T(8,128)} copy(f32[3,64,128]{2,1,0:T(8,128)} %render.1) | data formatting | bytes 196608

commit v4 on v3

--- a/solution.py
+++ b/solution.py
@@ -170,7 +170,7 @@
                 fld[z + 1, j + 1, 8 * g + 8 : 8 * g + 16, :] = raw[j, z, 8 * g : 8 * g + 8, :].astype(f32)
             return c
 
-        return lax.fori_loop(0, cells, layer, carry, unroll=2)
+        return lax.fori_loop(0, cells, layer, carry, unroll=8)
 
     lax.fori_loop(0, 4, take, 0)
 
@@ -310,7 +310,7 @@
         pk[rows, :] = packed
         return carry
 
-    lax.fori_loop(0, 8, finish, 0, unroll=2)
+    lax.fori_loop(0, 8, finish, 0, unroll=4)
 
     top, bottom = pl.ds(0, 8), pl.ds(72, 8)
     halo = [
@@ -368,7 +368,7 @@
             tot[c, rows_at(8 * g), :] = sums[c]
         return carry
 
-    lax.fori_loop(1, 9, shift_rows, 0, unroll=2)
+    lax.fori_loop(1, 9, shift_rows, 0, unroll=4)
     lax.fori_loop(1, 7, inside, 0)
     for copy in halo:
         copy.wait()
@@ -407,7 +407,7 @@
             rim[p, rows, :] = v
         return carry
 
-    lax.fori_loop(0, 10, rim_rows, 0, unroll=5)
+    lax.fori_loop(0, 10, rim_rows, 0, unroll=10)
 
     def outside(G, carry):
         groups = [4 * G + i for i in range(4)]
@@ -441,7 +441,7 @@
                 out_ref[c, rows_at(8 * g), :] = total[c] * inv
         return carry
 
-    lax.fori_loop(0, 2, outside, 0)
+    lax.fori_loop(0, 2, outside, 0, unroll=2)
     for s in range(4):
         to_sibling(s).wait_send()
     for s in range(3):

time: 51.7 us -> 51 us (0.986)
  Pallas kernels: 49.3 us -> 48.7 us
    pallas_call x1, Pallas kernels: 49.3 us -> 48.7 us  [per_device(): pl.pallas_call(kernel, out_shape=jax.ShapeDtypeStruct((3, 64, 128), f32),...]
where the time goes in v4:
time: 51 us; the launch traced here: 50.9 us
  Pallas kernels  48.7 us (95%)
  local copies, waits for them, and re-layouts  1.54 us (3%)
  between operations  0.66 us (1%)
    pallas_call x1, Pallas kernels, per_device(): pl.pallas_call(kernel, out_shape=jax.ShapeDtypeStruct((3, 64, 128), f32),...  48.7 us
    unnamed x1, local copies, waits for them, and re-layouts  1.54 us

profile of v4, /device:TPU:1, one launch (start us, length us, event | category | flops | bytes accessed | tf_op | source)
XLA Modules:
  0.0 50.9 jit_solution(7928862833439626751)
XLA Ops:
  0.7 48.7 %render.1 = f32[3,64,128]{2,1,0:T(8,128)} custom-call(s32[1]{0:T(128)S(6)} %copy.5.flip_ref, f32[4,4]{1,0:T(4,128)} %tf_ref.1, s32[32,64,1024]{2,1,0:T(8,128)} %dens.1), custom_call_target="tpu_custom_call" | custom-call | tf_op jit(solution)/shard_map/render/pallas_call | solution.py:455
  49.3 1.5 %copy.6 = f32[3,64,128]{2,1,0:T(8,128)} copy(f32[3,64,128]{2,1,0:T(8,128)} %render.1) | data formatting | bytes 196608
